TPU v7x, 128 devices: a whole 4x4x4 slice. The times are simulated.
128 devices in a mesh: region: 128 (over x, y, z, core).
Axes of the slice: x: 4, y: 4, z: 4, core: 2. Of those that a mesh axis runs over, the one named last changes fastest.
Arguments:
- node_feat: bfloat16 [65536, 512], P('region'), may hold values from -6 to 6
- edge_feat: bfloat16 [524288, 512], P('region'), may hold values from -6 to 6
- sender: int32 [524288], P('region'), may hold values from 0 to 2815, as said below
- receiver: int32 [524288], P('region'), may hold values from 0 to 512, as said below
- send_list: int32 [128, 8, 32], P('region'), may hold values from 16 to 511
- edge_w1: bfloat16 [1536, 512], replicated, may hold values from -0.15625 to 0.15625
- edge_b1: float32 [512], replicated, may hold values from -4 to 4
- edge_w2: bfloat16 [512, 512], replicated, may hold values from -0.25 to 0.25
- edge_b2: float32 [512], replicated, may hold values from -4 to 4
- edge_gain: float32 [512], replicated, may hold values from 0.5 to 1.5
- edge_shift: float32 [512], replicated, may hold values from -4 to 4
- node_w1: bfloat16 [1024, 512], replicated, may hold values from -0.1875 to 0.1875
- node_b1: float32 [512], replicated, may hold values from -4 to 4
- node_w2: bfloat16 [512, 512], replicated, may hold values from -0.25 to 0.25
- node_b2: float32 [512], replicated, may hold values from -4 to 4
- node_gain: float32 [512], replicated, may hold values from 0.5 to 1.5
- node_shift: float32 [512], replicated, may hold values from -4 to 4
Outputs:
- edge_out: bfloat16 [524288, 512], P('region')
- node_out: bfloat16 [65536, 512], P('region')
Inputs may be any that keep to these rules, and one draw needn't show every extreme that they name: `sender`: a row of the region's table as built in the first step; every region has slots pointing at row 0 and at the last row. `receiver`: non-decreasing within each region's 4096 slots; the value 512 marks an empty slot, and empty slots stand after the used ones; some region uses all its slots. `send_list`: entry [s, j, k] is a local index on region s of a node that s sends to its j-th neighbour.
All inputs are finite; a program needn't handle non-finite values.
Results may differ from a plain program's by a relative error of at most 0.0043.
Values may be sent and summed in bfloat16 or wider, within the bound.
No kernel may reach another device: no remote copies, remote signals or barrier semaphores. Data moves between devices by JAX's collectives and lax.ppermute only.
A program may use at most 128 MiB of HBM per device.

v0:
```python
import jax
import jax.numpy as jnp
from jax import lax
from jax.sharding import PartitionSpec as P

COARSE_DEV = 16
NEIGHBOUR_STEPS = (1, -1, 7, -7, 8, -8, 9, -9)


def from_behind(block, axis, distance):
    devices = range(lax.axis_size(axis))
    route = [((i - distance) % len(devices), i) for i in devices]
    return lax.ppermute(block, axis, route)


def finish(pre, w_second, b_second, gain, shift):
    hidden = jax.nn.silu(pre).astype(jnp.bfloat16)
    out = jnp.dot(hidden, w_second, preferred_element_type=jnp.float32) + b_second
    mean = jnp.mean(out, axis=-1, keepdims=True)
    var = jnp.mean((out - mean) ** 2, axis=-1, keepdims=True)
    return (out - mean) * lax.rsqrt(var + 1e-05) * gain + shift


def pick_rows(wanted_rows, source, block_size):
    total_rows = wanted_rows.shape[0]
    grouped = wanted_rows.reshape(total_rows // block_size, block_size)
    source_ids = jnp.arange(source.shape[0], dtype=jnp.int32)

    def select(group_rows):
        one_hot = (group_rows[:, None] == source_ids[None, :]).astype(source.dtype)
        return jnp.dot(one_hot, source, preferred_element_type=jnp.float32).astype(source.dtype)

    return lax.map(select, grouped).reshape(total_rows, source.shape[1])


def on_device(
    node_feat,
    edge_feat,
    sender,
    receiver,
    send_list,
    edge_w1,
    edge_b1,
    edge_w2,
    edge_b2,
    edge_gain,
    edge_shift,
    node_w1,
    node_b1,
    node_w2,
    node_b2,
    node_gain,
    node_shift,
):
    width = node_feat.shape[1]
    node_rows = node_feat.shape[0]
    edge_rows = edge_feat.shape[0]
    neighbours = send_list.shape[1]
    slots = send_list.shape[2]
    block_size = min(512, edge_rows)
    block_count = edge_rows // block_size
    coarse = node_feat[:COARSE_DEV]
    outgoing = jnp.take(node_feat, send_list[0].reshape(-1), axis=0).reshape(
        neighbours, slots, width
    )
    coarse_all = lax.all_gather(coarse, "region", axis=0, tiled=True)
    arrived = [
        from_behind(rows_out, "region", distance)
        for rows_out, distance in zip(list(outgoing), NEIGHBOUR_STEPS)
    ]
    halo = jnp.concatenate(arrived, axis=0)
    table = jnp.concatenate([node_feat, coarse_all, halo], axis=0)
    live = receiver < node_rows
    recv_index = jnp.minimum(receiver, node_rows - 1)
    sent_rows = pick_rows(sender, table, block_size)
    recv_rows = pick_rows(recv_index, node_feat, block_size)
    inputs = jnp.concatenate([edge_feat, sent_rows, recv_rows], axis=1)
    edge_pre = jnp.dot(inputs, edge_w1, preferred_element_type=jnp.float32) + edge_b1
    update = finish(edge_pre, edge_w2, edge_b2, edge_gain, edge_shift)
    edge_out = jnp.where(live[:, None], edge_feat.astype(jnp.float32) + update, 0.0).astype(
        jnp.bfloat16
    )
    node_ids = jnp.arange(node_rows, dtype=jnp.int32)

    def add_block(position, running):
        first_slot = position * block_size
        block_rows = lax.dynamic_slice_in_dim(edge_out, first_slot, block_size, 0)
        block_ids = lax.dynamic_slice_in_dim(receiver, first_slot, block_size, 0)
        one_hot = (node_ids[:, None] == block_ids[None, :]).astype(jnp.bfloat16)
        return running + jnp.dot(one_hot, block_rows, preferred_element_type=jnp.float32)

    summed = lax.fori_loop(0, block_count, add_block, jnp.zeros((node_rows, width), jnp.float32))
    aggregate = summed.astype(jnp.bfloat16)
    node_in = jnp.concatenate([node_feat, aggregate], axis=1)
    node_pre = jnp.dot(node_in, node_w1, preferred_element_type=jnp.float32) + node_b1
    node_update = finish(node_pre, node_w2, node_b2, node_gain, node_shift)
    node_out = (node_feat.astype(jnp.float32) + node_update).astype(jnp.bfloat16)
    return (edge_out, node_out)


def solution(mesh):
    in_specs = (
        P("region", None),
        P("region", None),
        P("region"),
        P("region"),
        P("region", None, None),
        P(),
        P(),
        P(),
        P(),
        P(),
        P(),
        P(),
        P(),
        P(),
        P(),
        P(),
        P(),
    )
    out_specs = (P("region", None), P("region", None))
    return jax.shard_map(
        on_device, mesh=mesh, in_specs=in_specs, out_specs=out_specs, check_vma=False
    )
```

profile of v0, /device:TPU:0, one launch (start us, length us, event | category | flops | bytes accessed | tf_op | source)
XLA Modules:
  0.0 195.6 jit_solution(12757138436500873263)
XLA Ops:
  7.2 1.4 slice.11
  10.2 2.3 %gather_fusion = bf16[256,512]{1,0:T(8,128)(2,1)S(1)} fusion(bf16[512,512]{1,0:T(8,128)(2,1)} %param.23, s32[1024]{0:T(1024)S(1)} %pad_clamp_fusion), kind=kCustom, calls=%fused_computation | custom fusion | bytes 525312 | tf_op jit(solution)/shard_map/jit(_take)/gather | solution.py:63
  12.8 8.3 %collective-permute-start.1 = (bf16[32,512]{1,0:T(8,128)(2,1)S(1)}, bf16[32,512]{1,0:T(8,128)(2,1)}, u32[]{:S(2)}, u32[]{:S(2)}) collective-permute-start(bf16[32,512]{1,0:T(8,128)(2,1)S(1)} %get-tuple-element.226), channel_id=1, source_target_pairs={{1,0},{2,1},{3,2},{4,3},{5,4},{6,5},{7,6},{8,7},{9,8},{10,9},{11,1... | collective-permute-start | bytes 98312 | tf_op jit(solution)/shard_map/ppermute | solution.py:13
  21.1 5.1 %collective-permute-start.3 = (bf16[32,512]{1,0:T(8,128)(2,1)S(1)}, bf16[32,512]{1,0:T(8,128)(2,1)S(1)}, u32[]{:S(2)}, u32[]{:S(2)}) collective-permute-start(bf16[32,512]{1,0:T(8,128)(2,1)S(1)} %get-tuple-element.224), channel_id=1, source_target_pairs={{7,0},{8,1},{9,2},{10,3},{11,4},{12,5},{13,6},{14,7},{15,8},{16,9}... | collective-permute-start | bytes 98312 | tf_op jit(solution)/shard_map/ppermute | solution.py:13
  26.2 2.0 %copy.20 = bf16[512,512]{0,1:T(8,128)(2,1)} copy(bf16[512,512]{1,0:T(8,128)(2,1)} %param.23) | data formatting | bytes 1048576 | tf_op args[0]
  28.3 6.4 %copy.19 = bf16[4096,512]{0,1:T(8,128)(2,1)} copy(bf16[4096,512]{1,0:T(8,128)(2,1)} %param.24) | data formatting | bytes 8388608 | tf_op args[1]
  35.5 2.3 %broadcast.84.clone = bf16[8,512,512]{2,1,0:T(8,128)(2,1)} broadcast(bf16[]{:T(256)} %constant.76.clone.1), dimensions={} | broadcast | bytes 4194306 | tf_op jit(solution)/shard_map/broadcast.9
  37.8 10.4 %while.37 = (s32[]{:T(128)}, bf16[8,512,512]{2,1,0:T(8,128)(2,1)}, s32[8,512]{1,0:T(8,128)S(1)}, bf16[512,512]{1,0:T(8,128)(2,1)S(1)}, s32[]{:T(128)}) while((s32[]{:T(128)}, bf16[8,512,512]{2,1,0:T(8,128)(2,1)}, s32[8,512]{1,0:T(8,128)S(1)}, bf16[512,512]{1,0:T(8,128)(2,1)S(1)}, s32[]{:T(128)}) %tuple.90), condition=%wide.region_3.4_spmd.clone, body=%wide.region_2.3_spmd.clone.sunk | while | flops 268959744 | bytes 1055297 | solution.py:33
  37.8 1.3 fusion.65
  39.2 1.3 fusion.65
  40.5 1.3 fusion.65
  41.8 1.3 fusion.65
  43.1 1.3 fusion.65
  44.4 1.3 fusion.65
  45.7 1.3 fusion.65
  47.0 1.3 fusion.65
  48.3 30.9 %all-gather.2.cloned.1.call-done = bf16[2048,512]{1,0:T(8,128)(2,1)} async-done(((bf16[16,512]{1,0:T(8,128)(2,1)}), bf16[2048,512]{1,0:T(8,128)(2,1)}) %all-gather.2.cloned.1.call-update) | async-done | bytes 2097168 | tf_op jit(solution)/shard_map/all_gather | solution.py:66
  79.1 3.1 %constant_dynamic-update-slice_fusion.8 = bf16[2816,512]{1,0:T(8,128)(2,1)} fusion(bf16[2816,512]{1,0:T(8,128)(2,1)} %constant_dynamic-update-slice_fusion.9, bf16[2048,512]{1,0:T(8,128)(2,1)} %all-gather.2.cloned.1.call-done), kind=kLoop, calls=%fused_computation.54 | loop fusion | bytes 4194304
  82.2 2.7 %collective-permute-start.5 = (bf16[32,512]{1,0:T(8,128)(2,1)S(1)}, bf16[32,512]{1,0:T(8,128)(2,1)S(1)}, u32[]{:S(2)}, u32[]{:S(2)}) collective-permute-start(bf16[32,512]{1,0:T(8,128)(2,1)S(1)} %get-tuple-element.222), channel_id=1, source_target_pairs={{8,0},{9,1},{10,2},{11,3},{12,4},{13,5},{14,6},{15,7},{16,8},{17,9... | collective-permute-start | bytes 98312 | tf_op jit(solution)/shard_map/ppermute | solution.py:13
  84.9 1.4 constant_dynamic-update-slice_fusion.7
  86.3 1.4 constant_dynamic-update-slice_fusion.6
  87.6 7.5 %collective-permute-start.7 = (bf16[32,512]{1,0:T(8,128)(2,1)S(1)}, bf16[32,512]{1,0:T(8,128)(2,1)S(1)}, u32[]{:S(2)}, u32[]{:S(2)}) collective-permute-start(bf16[32,512]{1,0:T(8,128)(2,1)S(1)} %get-tuple-element.220), channel_id=1, source_target_pairs={{9,0},{10,1},{11,2},{12,3},{13,4},{14,5},{15,6},{16,7},{17,8},{18,... | collective-permute-start | bytes 98312 | tf_op jit(solution)/shard_map/ppermute | solution.py:13
  95.1 1.4 constant_dynamic-update-slice_fusion.5
  99.5 2.3 %broadcast.84.clone.1 = bf16[8,512,512]{2,1,0:T(8,128)(2,1)} broadcast(bf16[]{:T(256)} %constant.76.clone.1), dimensions={} | broadcast | bytes 4194306 | tf_op jit(solution)/shard_map/broadcast.9
  101.8 34.7 %while.36 = (s32[]{:T(128)}, bf16[8,512,512]{2,1,0:T(8,128)(2,1)}, s32[8,512]{1,0:T(8,128)S(1)}, bf16[2816,512]{1,0:T(8,128)(2,1)}, s32[]{:T(128)}) while((s32[]{:T(128)}, bf16[8,512,512]{2,1,0:T(8,128)(2,1)}, s32[8,512]{1,0:T(8,128)S(1)}, bf16[2816,512]{1,0:T(8,128)(2,1)}, s32[]{:T(128)}) %tuple.82), condition=%wide.region_1.2_spmd.clone, body=%wide.region_0.1_spmd.clone.sunk | while | flops 1478098944 | bytes 3414593 | solution.py:33
  101.8 4.4 %fusion.63 = bf16[8,512,512]{2,1,0:T(8,128)(2,1)} fusion(bf16[8,512,512]{2,1,0:T(8,128)(2,1)} %get-tuple-element.328, s32[]{:T(128)} %get-tuple-element.327, bf16[2816,512]{1,0:T(8,128)(2,1)} %get-tuple-element.335, s32[512]{0:T(512)S(1)} %bitcast.34), kind=kOutput, calls=%fused_computation.9.clone.1 | convolution fusion | flops 1478098944 | bytes 3410432 | tf_op jit(solution)/shard_map/while/body/eval_jaxpr/dot_general | solution.py:31
  106.2 4.3 %fusion.63 = bf16[8,512,512]{2,1,0:T(8,128)(2,1)} fusion(bf16[8,512,512]{2,1,0:T(8,128)(2,1)} %get-tuple-element.328, s32[]{:T(128)} %get-tuple-element.327, bf16[2816,512]{1,0:T(8,128)(2,1)} %get-tuple-element.335, s32[512]{0:T(512)S(1)} %bitcast.34), kind=kOutput, calls=%fused_computation.9.clone.1 | convolution fusion | flops 1478098944 | bytes 3410432 | tf_op jit(solution)/shard_map/while/body/eval_jaxpr/dot_general | solution.py:31
  110.5 4.3 %fusion.63 = bf16[8,512,512]{2,1,0:T(8,128)(2,1)} fusion(bf16[8,512,512]{2,1,0:T(8,128)(2,1)} %get-tuple-element.328, s32[]{:T(128)} %get-tuple-element.327, bf16[2816,512]{1,0:T(8,128)(2,1)} %get-tuple-element.335, s32[512]{0:T(512)S(1)} %bitcast.34), kind=kOutput, calls=%fused_computation.9.clone.1 | convolution fusion | flops 1478098944 | bytes 3410432 | tf_op jit(solution)/shard_map/while/body/eval_jaxpr/dot_general | solution.py:31
  114.9 4.3 %fusion.63 = bf16[8,512,512]{2,1,0:T(8,128)(2,1)} fusion(bf16[8,512,512]{2,1,0:T(8,128)(2,1)} %get-tuple-element.328, s32[]{:T(128)} %get-tuple-element.327, bf16[2816,512]{1,0:T(8,128)(2,1)} %get-tuple-element.335, s32[512]{0:T(512)S(1)} %bitcast.34), kind=kOutput, calls=%fused_computation.9.clone.1 | convolution fusion | flops 1478098944 | bytes 3410432 | tf_op jit(solution)/shard_map/while/body/eval_jaxpr/dot_general | solution.py:31
  119.2 4.3 %fusion.63 = bf16[8,512,512]{2,1,0:T(8,128)(2,1)} fusion(bf16[8,512,512]{2,1,0:T(8,128)(2,1)} %get-tuple-element.328, s32[]{:T(128)} %get-tuple-element.327, bf16[2816,512]{1,0:T(8,128)(2,1)} %get-tuple-element.335, s32[512]{0:T(512)S(1)} %bitcast.34), kind=kOutput, calls=%fused_computation.9.clone.1 | convolution fusion | flops 1478098944 | bytes 3410432 | tf_op jit(solution)/shard_map/while/body/eval_jaxpr/dot_general | solution.py:31
  123.5 4.3 %fusion.63 = bf16[8,512,512]{2,1,0:T(8,128)(2,1)} fusion(bf16[8,512,512]{2,1,0:T(8,128)(2,1)} %get-tuple-element.328, s32[]{:T(128)} %get-tuple-element.327, bf16[2816,512]{1,0:T(8,128)(2,1)} %get-tuple-element.335, s32[512]{0:T(512)S(1)} %bitcast.34), kind=kOutput, calls=%fused_computation.9.clone.1 | convolution fusion | flops 1478098944 | bytes 3410432 | tf_op jit(solution)/shard_map/while/body/eval_jaxpr/dot_general | solution.py:31
  127.9 4.3 %fusion.63 = bf16[8,512,512]{2,1,0:T(8,128)(2,1)} fusion(bf16[8,512,512]{2,1,0:T(8,128)(2,1)} %get-tuple-element.328, s32[]{:T(128)} %get-tuple-element.327, bf16[2816,512]{1,0:T(8,128)(2,1)} %get-tuple-element.335, s32[512]{0:T(512)S(1)} %bitcast.34), kind=kOutput, calls=%fused_computation.9.clone.1 | convolution fusion | flops 1478098944 | bytes 3410432 | tf_op jit(solution)/shard_map/while/body/eval_jaxpr/dot_general | solution.py:31
  132.2 4.3 %fusion.63 = bf16[8,512,512]{2,1,0:T(8,128)(2,1)} fusion(bf16[8,512,512]{2,1,0:T(8,128)(2,1)} %get-tuple-element.328, s32[]{:T(128)} %get-tuple-element.327, bf16[2816,512]{1,0:T(8,128)(2,1)} %get-tuple-element.335, s32[512]{0:T(512)S(1)} %bitcast.34), kind=kOutput, calls=%fused_computation.9.clone.1 | convolution fusion | flops 1478098944 | bytes 3410432 | tf_op jit(solution)/shard_map/while/body/eval_jaxpr/dot_general | solution.py:31
  136.6 13.9 %add_reduce_fusion = (f32[4096]{0:T(1024)S(1)}, f32[4096,512]{0,1:T(8,128)}) fusion(f32[512]{0:T(512)S(1)} %copy-done.5, bf16[512,512]{1,0:T(8,128)(2,1)} %param.30, bf16[1536,512]{1,0:T(8,128)(2,1)S(1)} %copy-done, bf16[4096,512]{1,0:T(8,128)(2,1)} %bitcast.32, bf16[4096,512]{1,0:T(8,128)(2,1)} %bitcast.31, bf16[4096,512]{1,0:T(8,128)(2,1)} %param.24, ...), kind=kOutput, calls=%fused_computation.31 | convolution fusion | flops 8644456448 | bytes 23089152 | tf_op jit(solution)/shard_map/dot_general | solution.py:18
  150.5 4.9 %multiply_reduce_fusion = f32[4096]{0:T(1024)S(1)} fusion(f32[4096,512]{0,1:T(8,128)} %get-tuple-element.229, f32[4096]{0:T(1024)S(1)} %broadcast_multiply_fusion, f32[512]{0:T(512)S(1)} %copy-done.5), kind=kLoop, calls=%fused_computation.29 | loop fusion | flops 8384512 | bytes 8423424 | tf_op jit(solution)/shard_map/reduce_sum | solution.py:20
  156.3 6.5 %select_convert_fusion = bf16[4096,512]{0,1:T(8,128)(2,1)} fusion(bf16[4096,512]{0,1:T(8,128)(2,1)} %copy.19, f32[4096,512]{0,1:T(8,128)S(1)} %copy-done.1, f32[512]{0:T(512)S(1)} %copy-done.6, f32[512]{0:T(512)S(1)} %copy-done.7, f32[4096]{0:T(1024)S(1)} %add_rsqrt_fusion, f32[4096]{0:T(1024)S(1)} %broadcast_multiply_fusion, f32[512]{0:T(512)S(1)} %copy-done.5, ...), kind=kLoop, calls=%fused_computation.28 | loop fusion | flops 18874368 | bytes 16820224 | tf_op jit(solution)/shard_map/convert_element_type | solution.py:80
  162.8 6.4 %copy.22 = bf16[4096,512]{1,0:T(8,128)(2,1)} copy(bf16[4096,512]{0,1:T(8,128)(2,1)} %select_convert_fusion) | data formatting | bytes 8388608
  169.2 13.3 %while.38 = (s32[]{:T(128)}, f32[512,512]{1,0:T(8,128)S(1)}, s32[4096]{0:T(1024)S(1)}, bf16[4096,512]{1,0:T(8,128)(2,1)}, s32[]{:T(128)}, /*index=5*/s32[]{:T(128)}, s32[]{:T(128)}, s32[]{:T(128)}) while((s32[]{:T(128)}, f32[512,512]{1,0:T(8,128)S(1)}, s32[4096]{0:T(1024)S(1)}, bf16[4096,512]{1,0:T(8,128)(2,1)}, s32[]{:T(128)}, ...), condition=%wide.region_7.8_spmd.clone, body=%wide.region_6.7_spmd.clone.sunk | while | flops 269221888 | bytes 2627733 | solution.py:92
  169.2 1.6 convolution_add_fusion.4
  170.9 1.6 convolution_add_fusion.4
  172.6 1.6 convolution_add_fusion.4
  174.2 1.6 convolution_add_fusion.4
  175.9 1.6 convolution_add_fusion.4
  177.6 1.6 convolution_add_fusion.4
  179.2 1.6 convolution_add_fusion.4
  180.9 1.6 convolution_add_fusion.4
  183.4 2.8 %fusion.48 = (f32[512]{0:T(512)S(1)}, f32[512,512]{0,1:T(8,128)S(1)}) fusion(f32[512]{0:T(512)S(1)} %copy-done.11, bf16[512,512]{1,0:T(8,128)(2,1)} %param.36, bf16[1024,512]{1,0:T(8,128)(2,1)} %param.34, bf16[512,512]{1,0:T(8,128)(2,1)} %convert_element_type.36, bf16[512,512]{1,0:T(8,128)(2,1)S(1)} %get-tuple-element.362, f32[512]{0:T(512)S(1)} %copy-done.12), kind=kOutput, calls=%fused_computation.71 | convolution fusion | flops 809500160 | bytes 3676160 | tf_op jit(solution)/shard_map/dot_general | solution.py:18
  186.4 1.3 add_convert_fusion
  (89 shorter events, 9.5 us)
Async XLA Ops:
  7.2 129.4 %copy-start = (bf16[1536,512]{1,0:T(8,128)(2,1)S(1)}, bf16[1536,512]{1,0:T(8,128)(2,1)}, u32[]{:S(2)}) copy-start(bf16[1536,512]{1,0:T(8,128)(2,1)} %param.28) | copy-start | bytes 4718596
  7.2 21.0 %copy-start.4 = (s32[4096]{0:T(1024)S(1)}, s32[4096]{0:T(1024)}, u32[]{:S(2)}) copy-start(s32[4096]{0:T(1024)} %param.25) | copy-start | bytes 49156
  7.2 21.0 %copy-start.3 = (s32[4096]{0:T(1024)S(1)}, s32[4096]{0:T(1024)}, u32[]{:S(2)}) copy-start(s32[4096]{0:T(1024)} %param.26) | copy-start | bytes 49156
  7.2 71.9 %all-gather.2.cloned.1.call-start = ((), (), s32[]{:S(2)}) async-start(), calls=%async_computation | async-start | bytes 2113536 | tf_op jit(solution)/shard_map/all_gather | solution.py:66
  12.7 69.5 %collective-permute-start = (bf16[32,512]{1,0:T(8,128)(2,1)S(1)}, bf16[32,512]{1,0:T(8,128)(2,1)}, u32[]{:S(2)}, u32[]{:S(2)}) collective-permute-start(bf16[32,512]{1,0:T(8,128)(2,1)S(1)} %get-tuple-element.227), channel_id=1, source_target_pairs={{127,0},{0,1},{1,2},{2,3},{3,4},{4,5},{5,6},{6,7},{7,8},{8,9},{9,1... | collective-permute-start | bytes 98312 | tf_op jit(solution)/shard_map/ppermute | solution.py:13
  12.8 73.5 %collective-permute-start.1 = (bf16[32,512]{1,0:T(8,128)(2,1)S(1)}, bf16[32,512]{1,0:T(8,128)(2,1)}, u32[]{:S(2)}, u32[]{:S(2)}) collective-permute-start(bf16[32,512]{1,0:T(8,128)(2,1)S(1)} %get-tuple-element.226), channel_id=1, source_target_pairs={{1,0},{2,1},{3,2},{4,3},{5,4},{6,5},{7,6},{8,7},{9,8},{10,9},{11,1... | collective-permute-start | bytes 98312 | tf_op jit(solution)/shard_map/ppermute | solution.py:13
  21.1 66.5 %collective-permute-start.2 = (bf16[32,512]{1,0:T(8,128)(2,1)S(1)}, bf16[32,512]{1,0:T(8,128)(2,1)}, u32[]{:S(2)}, u32[]{:S(2)}) collective-permute-start(bf16[32,512]{1,0:T(8,128)(2,1)S(1)} %get-tuple-element.225), channel_id=1, source_target_pairs={{121,0},{122,1},{123,2},{124,3},{125,4},{126,5},{127,6},{0,7},{1,8... | collective-permute-start | bytes 98312 | tf_op jit(solution)/shard_map/ppermute | solution.py:13
  21.1 75.4 %collective-permute-start.3 = (bf16[32,512]{1,0:T(8,128)(2,1)S(1)}, bf16[32,512]{1,0:T(8,128)(2,1)S(1)}, u32[]{:S(2)}, u32[]{:S(2)}) collective-permute-start(bf16[32,512]{1,0:T(8,128)(2,1)S(1)} %get-tuple-element.224), channel_id=1, source_target_pairs={{7,0},{8,1},{9,2},{10,3},{11,4},{12,5},{13,6},{14,7},{15,8},{16,9}... | collective-permute-start | bytes 98312 | tf_op jit(solution)/shard_map/ppermute | solution.py:13
  26.2 70.9 %collective-permute-start.4 = (bf16[32,512]{1,0:T(8,128)(2,1)S(1)}, bf16[32,512]{1,0:T(8,128)(2,1)S(1)}, u32[]{:S(2)}, u32[]{:S(2)}) collective-permute-start(bf16[32,512]{1,0:T(8,128)(2,1)S(1)} %get-tuple-element.223), channel_id=1, source_target_pairs={{120,0},{121,1},{122,2},{123,3},{124,4},{125,5},{126,6},{127,7},{0... | collective-permute-start | bytes 98312 | tf_op jit(solution)/shard_map/ppermute | solution.py:13
  28.3 6.4 %copy-start.2 = (bf16[512,512]{1,0:T(8,128)(2,1)S(1)}, bf16[512,512]{1,0:T(8,128)(2,1)}, u32[]{:S(2)}) copy-start(bf16[512,512]{1,0:T(8,128)(2,1)} %param.23) | copy-start | bytes 1572868
  82.2 15.5 %collective-permute-start.5 = (bf16[32,512]{1,0:T(8,128)(2,1)S(1)}, bf16[32,512]{1,0:T(8,128)(2,1)S(1)}, u32[]{:S(2)}, u32[]{:S(2)}) collective-permute-start(bf16[32,512]{1,0:T(8,128)(2,1)S(1)} %get-tuple-element.222), channel_id=1, source_target_pairs={{8,0},{9,1},{10,2},{11,3},{12,4},{13,5},{14,6},{15,7},{16,8},{17,9... | collective-permute-start | bytes 98312 | tf_op jit(solution)/shard_map/ppermute | solution.py:13
  86.3 12.1 %collective-permute-start.6 = (bf16[32,512]{1,0:T(8,128)(2,1)S(1)}, bf16[32,512]{1,0:T(8,128)(2,1)S(1)}, u32[]{:S(2)}, u32[]{:S(2)}) collective-permute-start(bf16[32,512]{1,0:T(8,128)(2,1)S(1)} %get-tuple-element.221), channel_id=1, source_target_pairs={{119,0},{120,1},{121,2},{122,3},{123,4},{124,5},{125,6},{126,7},{1... | collective-permute-start | bytes 98312 | tf_op jit(solution)/shard_map/ppermute | solution.py:13
  87.6 11.3 %collective-permute-start.7 = (bf16[32,512]{1,0:T(8,128)(2,1)S(1)}, bf16[32,512]{1,0:T(8,128)(2,1)S(1)}, u32[]{:S(2)}, u32[]{:S(2)}) collective-permute-start(bf16[32,512]{1,0:T(8,128)(2,1)S(1)} %get-tuple-element.220), channel_id=1, source_target_pairs={{9,0},{10,1},{11,2},{12,3},{13,4},{14,5},{15,6},{16,7},{17,8},{18,... | collective-permute-start | bytes 98312 | tf_op jit(solution)/shard_map/ppermute | solution.py:13
  101.8 34.7 %copy-start.5 = (f32[512]{0:T(512)S(1)}, f32[512]{0:T(512)}, u32[]{:S(2)}) copy-start(f32[512]{0:T(512)} %param.31) | copy-start | bytes 6148
  101.8 34.7 %copy-start.10 = (f32[512]{0:T(512)S(1)}, f32[512]{0:T(512)}, u32[]{:S(2)}) copy-start(f32[512]{0:T(512)} %param.29) | copy-start | bytes 6148
  150.5 5.8 %copy-start.1 = (f32[4096,512]{0,1:T(8,128)S(1)}, f32[4096,512]{0,1:T(8,128)}, u32[]{:S(2)}) copy-start(f32[4096,512]{0,1:T(8,128)} %get-tuple-element.229) | copy-start | bytes 25165828
  150.5 5.8 %copy-start.6 = (f32[512]{0:T(512)S(1)}, f32[512]{0:T(512)}, u32[]{:S(2)}) copy-start(f32[512]{0:T(512)} %param.33) | copy-start | bytes 6148
  150.5 5.8 %copy-start.7 = (f32[512]{0:T(512)S(1)}, f32[512]{0:T(512)}, u32[]{:S(2)}) copy-start(f32[512]{0:T(512)} %param.32) | copy-start | bytes 6148
  169.2 14.2 %copy-start.11 = (f32[512]{0:T(512)S(1)}, f32[512]{0:T(512)}, u32[]{:S(2)}) copy-start(f32[512]{0:T(512)} %param.37) | copy-start | bytes 6148
  169.2 14.2 %copy-start.12 = (f32[512]{0:T(512)S(1)}, f32[512]{0:T(512)}, u32[]{:S(2)}) copy-start(f32[512]{0:T(512)} %param.35) | copy-start | bytes 6148
  183.4 3.0 %copy-start.8 = (f32[512]{0:T(512)S(1)}, f32[512]{0:T(512)}, u32[]{:S(2)}) copy-start(f32[512]{0:T(512)} %param.39) | copy-start | bytes 6148
  183.4 3.0 %copy-start.9 = (f32[512]{0:T(512)S(1)}, f32[512]{0:T(512)}, u32[]{:S(2)}) copy-start(f32[512]{0:T(512)} %param.38) | copy-start | bytes 6148
Sparse Core Ops, SparseCore 0:
  11.1 67.9 all-gather.1
where the time goes:
time: 197 us; the launch traced here: 196 us
  matrix products  74.3 us (38%)
  local copies, waits for them, and re-layouts  38.4 us (19%)
  waiting for transfers between devices  30.9 us (16%)
  starting transfers between devices  23.6 us (12%)
  between operations  14.2 us (7%)
  other arithmetic  13.9 us (7%)
    dot_general x16, matrix products, select(): jnp.dot(one_hot, source, preferred_element_type=jnp.float32)  45.1 us
    all_gather x1, waiting for transfers between devices, on_device(): coarse_all = lax.all_gather(coarse, 'region', axis=0, tiled=True)  30.9 us
    unnamed x39, local copies, waits for them, and re-layouts  27.2 us
    ppermute x8, starting transfers between devices, from_behind(): return lax.ppermute(block, axis, route)  23.6 us
    dot_general x2, matrix products, finish(): jnp.dot(hidden, w_second, preferred_element_type=jnp.float32) + b_second  16.7 us
    dot_general x8, matrix products, add_block(): jnp.dot(one_hot, block_rows, preferred_element_type=jnp.float32)  12.5 us
    convert_element_type x1, other arithmetic, on_device(): jnp.where(live[:, None], edge_feat.astype(jnp.float32) + update, 0.0)  6.49 us
    reduce_sum x2, other arithmetic, finish(): var = jnp.mean((out - mean) ** 2, axis=-1, keepdims=True)  5.06 us
  transfers between devices with their start and end apart: 9, of which 1 were waited for; matrix products, arithmetic and copies ran while one was open for 18% of the time, Pallas kernels for 0%

commit v1 on v0

--- a/solution.py
+++ b/solution.py
@@ -63,7 +63,8 @@
     outgoing = jnp.take(node_feat, send_list[0].reshape(-1), axis=0).reshape(
         neighbours, slots, width
     )
-    coarse_all = lax.all_gather(coarse, "region", axis=0, tiled=True)
+    stack = jnp.stack([coarse] * lax.axis_size("region"))
+    coarse_all = jnp.concatenate(lax.all_to_all(stack, "region", 0, 0), axis=0)
     arrived = [
         from_behind(rows_out, "region", distance)
         for rows_out, distance in zip(list(outgoing), NEIGHBOUR_STEPS)

time: 197 us -> 167 us (0.85)
  waiting for transfers between devices: 30.9 us -> 0.02 us
  starting transfers between devices: 23.6 us -> 37.9 us
  between operations: 14.2 us -> 0.82 us
    all_gather x1 -> x0, waiting for transfers between devices: 30.9 us -> none  [on_device(): coarse_all = lax.all_gather(coarse, 'region', axis=0, tiled=True)]
    all_to_all x0 -> x1, starting transfers between devices: none -> 12.9 us  [on_device(): coarse_all = jnp.concatenate(lax.all_to_all(stack, 'region', 0, 0), axis=0)]
    another operation x2 -> x3, local copies, waits for them, and re-layouts: 4.61 us -> 6.25 us
  transfers between devices with their start and end apart: 9 -> 9, of which waited for: 1 -> 0; matrix products, arithmetic and copies ran while one was open for 18% -> 20% of each run, Pallas kernels for 0% -> 0%
where the time goes in v1:
time: 167 us; the launch traced here: 165 us
  matrix products  74.2 us (44%)
  local copies, waits for them, and re-layouts  38.3 us (23%)
  starting transfers between devices  37.9 us (23%)
  other arithmetic  13.9 us (8%)
    dot_general x16, matrix products, select(): jnp.dot(one_hot, source, preferred_element_type=jnp.float32)  45 us
    unnamed x39, local copies, waits for them, and re-layouts  26 us
    ppermute x8, starting transfers between devices, from_behind(): return lax.ppermute(block, axis, route)  25 us
    dot_general x2, matrix products, finish(): jnp.dot(hidden, w_second, preferred_element_type=jnp.float32) + b_second  16.6 us
    all_to_all x1, starting transfers between devices, on_device(): coarse_all = jnp.concatenate(lax.all_to_all(stack, 'region', 0, 0), axis=0)  12.9 us
    dot_general x8, matrix products, add_block(): jnp.dot(one_hot, block_rows, preferred_element_type=jnp.float32)  12.5 us
    convert_element_type x1, other arithmetic, on_device(): jnp.where(live[:, None], edge_feat.astype(jnp.float32) + update, 0.0)  6.49 us
    reduce_sum x2, other arithmetic, finish(): var = jnp.mean((out - mean) ** 2, axis=-1, keepdims=True)  5.06 us
  transfers between devices with their start and end apart: 9, of which 0 were waited for; matrix products, arithmetic and copies ran while one was open for 20% of the time, Pallas kernels for 0%

profile of v1, /device:TPU:0, one launch (start us, length us, event | category | flops | bytes accessed | tf_op | source)
XLA Modules:
  0.0 165.3 jit_solution(4054139315689755106)
XLA Ops:
  2.3 2.3 %gather_fusion = bf16[256,512]{1,0:T(8,128)(2,1)S(1)} fusion(bf16[512,512]{1,0:T(8,128)(2,1)} %param.23, s32[1024]{0:T(1024)S(1)} %pad_clamp_fusion), kind=kCustom, calls=%fused_computation | custom fusion | bytes 525312 | tf_op jit(solution)/shard_map/jit(_take)/gather | solution.py:63
  5.6 1.6 stack.2
  7.2 12.9 %all-to-all-start = ((bf16[128,16,512]{2,1,0:T(8,128)(2,1)}), bf16[128,16,512]{2,1,0:T(8,128)(2,1)}, u32[]{:S(2)}, u32[]{:S(2)}) async-start(bf16[128,16,512]{2,1,0:T(8,128)(2,1)} %stack.2), calls=%async_computation | async-start | bytes 4194304 | tf_op jit(solution)/shard_map/all_to_all | solution.py:67
  20.1 7.0 %collective-permute-start.1 = (bf16[32,512]{1,0:T(8,128)(2,1)S(1)}, bf16[32,512]{1,0:T(8,128)(2,1)}, u32[]{:S(2)}, u32[]{:S(2)}) collective-permute-start(bf16[32,512]{1,0:T(8,128)(2,1)S(1)} %get-tuple-element.226), channel_id=1, source_target_pairs={{1,0},{2,1},{3,2},{4,3},{5,4},{6,5},{7,6},{8,7},{9,8},{10,9},{11,1... | collective-permute-start | bytes 98312 | tf_op jit(solution)/shard_map/ppermute | solution.py:13
  27.2 5.1 %collective-permute-start.3 = (bf16[32,512]{1,0:T(8,128)(2,1)S(1)}, bf16[32,512]{1,0:T(8,128)(2,1)S(1)}, u32[]{:S(2)}, u32[]{:S(2)}) collective-permute-start(bf16[32,512]{1,0:T(8,128)(2,1)S(1)} %get-tuple-element.224), channel_id=1, source_target_pairs={{7,0},{8,1},{9,2},{10,3},{11,4},{12,5},{13,6},{14,7},{15,8},{16,9}... | collective-permute-start | bytes 98312 | tf_op jit(solution)/shard_map/ppermute | solution.py:13
  33.1 1.0 copy.20
  34.1 6.3 %copy.19 = bf16[4096,512]{0,1:T(8,128)(2,1)} copy(bf16[4096,512]{1,0:T(8,128)(2,1)} %param.24) | data formatting | bytes 8388608 | tf_op args[1]
  40.4 2.3 %broadcast.86.clone = bf16[8,512,512]{2,1,0:T(8,128)(2,1)} broadcast(bf16[]{:T(256)} %constant.76.clone.1), dimensions={} | broadcast | bytes 4194306 | tf_op jit(solution)/shard_map/broadcast.9
  42.7 10.4 %while.37 = (s32[]{:T(128)}, bf16[8,512,512]{2,1,0:T(8,128)(2,1)}, s32[8,512]{1,0:T(8,128)S(1)}, bf16[512,512]{1,0:T(8,128)(2,1)S(1)}, s32[]{:T(128)}) while((s32[]{:T(128)}, bf16[8,512,512]{2,1,0:T(8,128)(2,1)}, s32[8,512]{1,0:T(8,128)S(1)}, bf16[512,512]{1,0:T(8,128)(2,1)S(1)}, s32[]{:T(128)}) %tuple.88), condition=%wide.region_3.4_spmd.clone, body=%wide.region_2.3_spmd.clone.sunk | while | flops 268959744 | bytes 1055297 | solution.py:33
  42.8 1.3 fusion.65
  44.1 1.3 fusion.65
  45.4 1.3 fusion.65
  46.7 1.3 fusion.65
  48.0 1.3 fusion.65
  49.3 1.3 fusion.65
  50.6 1.3 fusion.65
  51.9 1.3 fusion.65
  53.2 3.1 %constant_dynamic-update-slice_fusion.8 = bf16[2816,512]{1,0:T(8,128)(2,1)} fusion(bf16[2816,512]{1,0:T(8,128)(2,1)} %constant_dynamic-update-slice_fusion.9, bf16[2048,512]{1,0:T(8,128)(2,1)} %bitcast), kind=kLoop, calls=%fused_computation.54 | loop fusion | bytes 4194304
  56.3 5.4 %collective-permute-start.5 = (bf16[32,512]{1,0:T(8,128)(2,1)S(1)}, bf16[32,512]{1,0:T(8,128)(2,1)S(1)}, u32[]{:S(2)}, u32[]{:S(2)}) collective-permute-start(bf16[32,512]{1,0:T(8,128)(2,1)S(1)} %get-tuple-element.222), channel_id=1, source_target_pairs={{8,0},{9,1},{10,2},{11,3},{12,4},{13,5},{14,6},{15,7},{16,8},{17,9... | collective-permute-start | bytes 98312 | tf_op jit(solution)/shard_map/ppermute | solution.py:13
  61.6 1.4 constant_dynamic-update-slice_fusion.7
  63.0 1.4 constant_dynamic-update-slice_fusion.6
  64.3 7.5 %collective-permute-start.7 = (bf16[32,512]{1,0:T(8,128)(2,1)S(1)}, bf16[32,512]{1,0:T(8,128)(2,1)S(1)}, u32[]{:S(2)}, u32[]{:S(2)}) collective-permute-start(bf16[32,512]{1,0:T(8,128)(2,1)S(1)} %get-tuple-element.220), channel_id=1, source_target_pairs={{9,0},{10,1},{11,2},{12,3},{13,4},{14,5},{15,6},{16,7},{17,8},{18,... | collective-permute-start | bytes 98312 | tf_op jit(solution)/shard_map/ppermute | solution.py:13
  71.8 1.4 constant_dynamic-update-slice_fusion.5
  76.2 2.3 %broadcast.86.clone.1 = bf16[8,512,512]{2,1,0:T(8,128)(2,1)} broadcast(bf16[]{:T(256)} %constant.76.clone.1), dimensions={} | broadcast | bytes 4194306 | tf_op jit(solution)/shard_map/broadcast.9
  78.5 34.7 %while.36 = (s32[]{:T(128)}, bf16[8,512,512]{2,1,0:T(8,128)(2,1)}, s32[8,512]{1,0:T(8,128)S(1)}, bf16[2816,512]{1,0:T(8,128)(2,1)}, s32[]{:T(128)}) while((s32[]{:T(128)}, bf16[8,512,512]{2,1,0:T(8,128)(2,1)}, s32[8,512]{1,0:T(8,128)S(1)}, bf16[2816,512]{1,0:T(8,128)(2,1)}, s32[]{:T(128)}) %tuple.82), condition=%wide.region_1.2_spmd.clone, body=%wide.region_0.1_spmd.clone.sunk | while | flops 1478098944 | bytes 3414593 | solution.py:33
  78.5 4.4 %fusion.63 = bf16[8,512,512]{2,1,0:T(8,128)(2,1)} fusion(bf16[8,512,512]{2,1,0:T(8,128)(2,1)} %get-tuple-element.328, s32[]{:T(128)} %get-tuple-element.327, bf16[2816,512]{1,0:T(8,128)(2,1)} %get-tuple-element.335, s32[512]{0:T(512)S(1)} %bitcast.35), kind=kOutput, calls=%fused_computation.9.clone.1 | convolution fusion | flops 1478098944 | bytes 3410432 | tf_op jit(solution)/shard_map/while/body/eval_jaxpr/dot_general | solution.py:31
  82.9 4.3 %fusion.63 = bf16[8,512,512]{2,1,0:T(8,128)(2,1)} fusion(bf16[8,512,512]{2,1,0:T(8,128)(2,1)} %get-tuple-element.328, s32[]{:T(128)} %get-tuple-element.327, bf16[2816,512]{1,0:T(8,128)(2,1)} %get-tuple-element.335, s32[512]{0:T(512)S(1)} %bitcast.35), kind=kOutput, calls=%fused_computation.9.clone.1 | convolution fusion | flops 1478098944 | bytes 3410432 | tf_op jit(solution)/shard_map/while/body/eval_jaxpr/dot_general | solution.py:31
  87.2 4.3 %fusion.63 = bf16[8,512,512]{2,1,0:T(8,128)(2,1)} fusion(bf16[8,512,512]{2,1,0:T(8,128)(2,1)} %get-tuple-element.328, s32[]{:T(128)} %get-tuple-element.327, bf16[2816,512]{1,0:T(8,128)(2,1)} %get-tuple-element.335, s32[512]{0:T(512)S(1)} %bitcast.35), kind=kOutput, calls=%fused_computation.9.clone.1 | convolution fusion | flops 1478098944 | bytes 3410432 | tf_op jit(solution)/shard_map/while/body/eval_jaxpr/dot_general | solution.py:31
  91.5 4.3 %fusion.63 = bf16[8,512,512]{2,1,0:T(8,128)(2,1)} fusion(bf16[8,512,512]{2,1,0:T(8,128)(2,1)} %get-tuple-element.328, s32[]{:T(128)} %get-tuple-element.327, bf16[2816,512]{1,0:T(8,128)(2,1)} %get-tuple-element.335, s32[512]{0:T(512)S(1)} %bitcast.35), kind=kOutput, calls=%fused_computation.9.clone.1 | convolution fusion | flops 1478098944 | bytes 3410432 | tf_op jit(solution)/shard_map/while/body/eval_jaxpr/dot_general | solution.py:31
  95.9 4.3 %fusion.63 = bf16[8,512,512]{2,1,0:T(8,128)(2,1)} fusion(bf16[8,512,512]{2,1,0:T(8,128)(2,1)} %get-tuple-element.328, s32[]{:T(128)} %get-tuple-element.327, bf16[2816,512]{1,0:T(8,128)(2,1)} %get-tuple-element.335, s32[512]{0:T(512)S(1)} %bitcast.35), kind=kOutput, calls=%fused_computation.9.clone.1 | convolution fusion | flops 1478098944 | bytes 3410432 | tf_op jit(solution)/shard_map/while/body/eval_jaxpr/dot_general | solution.py:31
  100.2 4.3 %fusion.63 = bf16[8,512,512]{2,1,0:T(8,128)(2,1)} fusion(bf16[8,512,512]{2,1,0:T(8,128)(2,1)} %get-tuple-element.328, s32[]{:T(128)} %get-tuple-element.327, bf16[2816,512]{1,0:T(8,128)(2,1)} %get-tuple-element.335, s32[512]{0:T(512)S(1)} %bitcast.35), kind=kOutput, calls=%fused_computation.9.clone.1 | convolution fusion | flops 1478098944 | bytes 3410432 | tf_op jit(solution)/shard_map/while/body/eval_jaxpr/dot_general | solution.py:31
  104.5 4.3 %fusion.63 = bf16[8,512,512]{2,1,0:T(8,128)(2,1)} fusion(bf16[8,512,512]{2,1,0:T(8,128)(2,1)} %get-tuple-element.328, s32[]{:T(128)} %get-tuple-element.327, bf16[2816,512]{1,0:T(8,128)(2,1)} %get-tuple-element.335, s32[512]{0:T(512)S(1)} %bitcast.35), kind=kOutput, calls=%fused_computation.9.clone.1 | convolution fusion | flops 1478098944 | bytes 3410432 | tf_op jit(solution)/shard_map/while/body/eval_jaxpr/dot_general | solution.py:31
  108.9 4.3 %fusion.63 = bf16[8,512,512]{2,1,0:T(8,128)(2,1)} fusion(bf16[8,512,512]{2,1,0:T(8,128)(2,1)} %get-tuple-element.328, s32[]{:T(128)} %get-tuple-element.327, bf16[2816,512]{1,0:T(8,128)(2,1)} %get-tuple-element.335, s32[512]{0:T(512)S(1)} %bitcast.35), kind=kOutput, calls=%fused_computation.9.clone.1 | convolution fusion | flops 1478098944 | bytes 3410432 | tf_op jit(solution)/shard_map/while/body/eval_jaxpr/dot_general | solution.py:31
  113.2 13.8 %add_reduce_fusion = (f32[4096]{0:T(1024)S(1)}, f32[4096,512]{0,1:T(8,128)}) fusion(f32[512]{0:T(512)S(1)} %copy-done.5, bf16[512,512]{1,0:T(8,128)(2,1)} %param.30, bf16[1536,512]{1,0:T(8,128)(2,1)S(1)} %copy-done, bf16[4096,512]{1,0:T(8,128)(2,1)} %bitcast.33, bf16[4096,512]{1,0:T(8,128)(2,1)} %bitcast.32, bf16[4096,512]{1,0:T(8,128)(2,1)} %param.24, ...), kind=kOutput, calls=%fused_computation.31 | convolution fusion | flops 8644456448 | bytes 23089152 | tf_op jit(solution)/shard_map/dot_general | solution.py:18
  127.1 4.9 %multiply_reduce_fusion = f32[4096]{0:T(1024)S(1)} fusion(f32[4096,512]{0,1:T(8,128)} %get-tuple-element.229, f32[4096]{0:T(1024)S(1)} %broadcast_multiply_fusion, f32[512]{0:T(512)S(1)} %copy-done.5), kind=kLoop, calls=%fused_computation.29 | loop fusion | flops 8384512 | bytes 8423424 | tf_op jit(solution)/shard_map/reduce_sum | solution.py:20
  132.8 6.5 %select_convert_fusion = bf16[4096,512]{0,1:T(8,128)(2,1)} fusion(bf16[4096,512]{0,1:T(8,128)(2,1)} %copy.19, f32[4096,512]{0,1:T(8,128)S(1)} %copy-done.1, f32[512]{0:T(512)S(1)} %copy-done.6, f32[512]{0:T(512)S(1)} %copy-done.7, f32[4096]{0:T(1024)S(1)} %add_rsqrt_fusion, f32[4096]{0:T(1024)S(1)} %broadcast_multiply_fusion, f32[512]{0:T(512)S(1)} %copy-done.5, ...), kind=kLoop, calls=%fused_computation.28 | loop fusion | flops 18874368 | bytes 16820224 | tf_op jit(solution)/shard_map/convert_element_type | solution.py:81
  139.3 6.4 %copy.22 = bf16[4096,512]{1,0:T(8,128)(2,1)} copy(bf16[4096,512]{0,1:T(8,128)(2,1)} %select_convert_fusion) | data formatting | bytes 8388608
  145.7 13.3 %while.38 = (s32[]{:T(128)}, f32[512,512]{1,0:T(8,128)S(1)}, s32[4096]{0:T(1024)S(1)}, bf16[4096,512]{1,0:T(8,128)(2,1)}, s32[]{:T(128)}, /*index=5*/s32[]{:T(128)}, s32[]{:T(128)}, s32[]{:T(128)}) while((s32[]{:T(128)}, f32[512,512]{1,0:T(8,128)S(1)}, s32[4096]{0:T(1024)S(1)}, bf16[4096,512]{1,0:T(8,128)(2,1)}, s32[]{:T(128)}, ...), condition=%wide.region_7.8_spmd.clone, body=%wide.region_6.7_spmd.clone.sunk | while | flops 269221888 | bytes 2627733 | solution.py:93
  145.8 1.6 convolution_add_fusion.4
  147.5 1.6 convolution_add_fusion.4
  149.2 1.6 convolution_add_fusion.4
  150.8 1.6 convolution_add_fusion.4
  152.5 1.6 convolution_add_fusion.4
  154.2 1.6 convolution_add_fusion.4
  155.8 1.6 convolution_add_fusion.4
  157.5 1.6 convolution_add_fusion.4
  160.0 2.8 %fusion.48 = (f32[512]{0:T(512)S(1)}, f32[512,512]{0,1:T(8,128)S(1)}) fusion(f32[512]{0:T(512)S(1)} %copy-done.11, bf16[512,512]{1,0:T(8,128)(2,1)} %param.36, bf16[1024,512]{1,0:T(8,128)(2,1)} %param.34, bf16[512,512]{1,0:T(8,128)(2,1)} %convert_element_type.36, bf16[512,512]{1,0:T(8,128)(2,1)S(1)} %get-tuple-element.361, f32[512]{0:T(512)S(1)} %copy-done.12), kind=kOutput, calls=%fused_computation.71 | convolution fusion | flops 809500160 | bytes 3676160 | tf_op jit(solution)/shard_map/dot_general | solution.py:18
  163.0 1.3 add_convert_fusion
  (89 shorter events, 10.2 us)
Async XLA Ops:
  0.6 112.6 %copy-start = (bf16[1536,512]{1,0:T(8,128)(2,1)S(1)}, bf16[1536,512]{1,0:T(8,128)(2,1)}, u32[]{:S(2)}) copy-start(bf16[1536,512]{1,0:T(8,128)(2,1)} %param.28) | copy-start | bytes 4718596
  4.6 27.6 %copy-start.2 = (bf16[512,512]{1,0:T(8,128)(2,1)S(1)}, bf16[512,512]{1,0:T(8,128)(2,1)}, u32[]{:S(2)}) copy-start(bf16[512,512]{1,0:T(8,128)(2,1)} %param.23) | copy-start | bytes 1572868
  4.7 28.4 %copy-start.3 = (s32[4096]{0:T(1024)S(1)}, s32[4096]{0:T(1024)}, u32[]{:S(2)}) copy-start(s32[4096]{0:T(1024)} %param.26) | copy-start | bytes 49156
  4.8 51.4 %collective-permute-start = (bf16[32,512]{1,0:T(8,128)(2,1)S(1)}, bf16[32,512]{1,0:T(8,128)(2,1)}, u32[]{:S(2)}, u32[]{:S(2)}) collective-permute-start(bf16[32,512]{1,0:T(8,128)(2,1)S(1)} %get-tuple-element.227), channel_id=1, source_target_pairs={{127,0},{0,1},{1,2},{2,3},{3,4},{4,5},{5,6},{6,7},{7,8},{8,9},{9,1... | collective-permute-start | bytes 98312 | tf_op jit(solution)/shard_map/ppermute | solution.py:13
  5.6 28.5 %copy-start.4 = (s32[4096]{0:T(1024)S(1)}, s32[4096]{0:T(1024)}, u32[]{:S(2)}) copy-start(s32[4096]{0:T(1024)} %param.25) | copy-start | bytes 49156
  7.2 45.9 %all-to-all-start = ((bf16[128,16,512]{2,1,0:T(8,128)(2,1)}), bf16[128,16,512]{2,1,0:T(8,128)(2,1)}, u32[]{:S(2)}, u32[]{:S(2)}) async-start(bf16[128,16,512]{2,1,0:T(8,128)(2,1)} %stack.2), calls=%async_computation | async-start | bytes 4194304 | tf_op jit(solution)/shard_map/all_to_all | solution.py:67
  20.1 42.8 %collective-permute-start.1 = (bf16[32,512]{1,0:T(8,128)(2,1)S(1)}, bf16[32,512]{1,0:T(8,128)(2,1)}, u32[]{:S(2)}, u32[]{:S(2)}) collective-permute-start(bf16[32,512]{1,0:T(8,128)(2,1)S(1)} %get-tuple-element.226), channel_id=1, source_target_pairs={{1,0},{2,1},{3,2},{4,3},{5,4},{6,5},{7,6},{8,7},{9,8},{10,9},{11,1... | collective-permute-start | bytes 98312 | tf_op jit(solution)/shard_map/ppermute | solution.py:13
  27.1 37.2 %collective-permute-start.2 = (bf16[32,512]{1,0:T(8,128)(2,1)S(1)}, bf16[32,512]{1,0:T(8,128)(2,1)}, u32[]{:S(2)}, u32[]{:S(2)}) collective-permute-start(bf16[32,512]{1,0:T(8,128)(2,1)S(1)} %get-tuple-element.225), channel_id=1, source_target_pairs={{121,0},{122,1},{123,2},{124,3},{125,4},{126,5},{127,6},{0,7},{1,8... | collective-permute-start | bytes 98312 | tf_op jit(solution)/shard_map/ppermute | solution.py:13
  27.2 46.0 %collective-permute-start.3 = (bf16[32,512]{1,0:T(8,128)(2,1)S(1)}, bf16[32,512]{1,0:T(8,128)(2,1)S(1)}, u32[]{:S(2)}, u32[]{:S(2)}) collective-permute-start(bf16[32,512]{1,0:T(8,128)(2,1)S(1)} %get-tuple-element.224), channel_id=1, source_target_pairs={{7,0},{8,1},{9,2},{10,3},{11,4},{12,5},{13,6},{14,7},{15,8},{16,9}... | collective-permute-start | bytes 98312 | tf_op jit(solution)/shard_map/ppermute | solution.py:13
  32.2 41.6 %collective-permute-start.4 = (bf16[32,512]{1,0:T(8,128)(2,1)S(1)}, bf16[32,512]{1,0:T(8,128)(2,1)S(1)}, u32[]{:S(2)}, u32[]{:S(2)}) collective-permute-start(bf16[32,512]{1,0:T(8,128)(2,1)S(1)} %get-tuple-element.223), channel_id=1, source_target_pairs={{120,0},{121,1},{122,2},{123,3},{124,4},{125,5},{126,6},{127,7},{0... | collective-permute-start | bytes 98312 | tf_op jit(solution)/shard_map/ppermute | solution.py:13
  56.3 18.1 %collective-permute-start.5 = (bf16[32,512]{1,0:T(8,128)(2,1)S(1)}, bf16[32,512]{1,0:T(8,128)(2,1)S(1)}, u32[]{:S(2)}, u32[]{:S(2)}) collective-permute-start(bf16[32,512]{1,0:T(8,128)(2,1)S(1)} %get-tuple-element.222), channel_id=1, source_target_pairs={{8,0},{9,1},{10,2},{11,3},{12,4},{13,5},{14,6},{15,7},{16,8},{17,9... | collective-permute-start | bytes 98312 | tf_op jit(solution)/shard_map/ppermute | solution.py:13
  63.0 12.0 %collective-permute-start.6 = (bf16[32,512]{1,0:T(8,128)(2,1)S(1)}, bf16[32,512]{1,0:T(8,128)(2,1)S(1)}, u32[]{:S(2)}, u32[]{:S(2)}) collective-permute-start(bf16[32,512]{1,0:T(8,128)(2,1)S(1)} %get-tuple-element.221), channel_id=1, source_target_pairs={{119,0},{120,1},{121,2},{122,3},{123,4},{124,5},{125,6},{126,7},{1... | collective-permute-start | bytes 98312 | tf_op jit(solution)/shard_map/ppermute | solution.py:13
  64.3 11.3 %collective-permute-start.7 = (bf16[32,512]{1,0:T(8,128)(2,1)S(1)}, bf16[32,512]{1,0:T(8,128)(2,1)S(1)}, u32[]{:S(2)}, u32[]{:S(2)}) collective-permute-start(bf16[32,512]{1,0:T(8,128)(2,1)S(1)} %get-tuple-element.220), channel_id=1, source_target_pairs={{9,0},{10,1},{11,2},{12,3},{13,4},{14,5},{15,6},{16,7},{17,8},{18,... | collective-permute-start | bytes 98312 | tf_op jit(solution)/shard_map/ppermute | solution.py:13
  78.5 34.7 %copy-start.5 = (f32[512]{0:T(512)S(1)}, f32[512]{0:T(512)}, u32[]{:S(2)}) copy-start(f32[512]{0:T(512)} %param.31) | copy-start | bytes 6148
  78.5 34.7 %copy-start.10 = (f32[512]{0:T(512)S(1)}, f32[512]{0:T(512)}, u32[]{:S(2)}) copy-start(f32[512]{0:T(512)} %param.29) | copy-start | bytes 6148
  127.1 5.8 %copy-start.1 = (f32[4096,512]{0,1:T(8,128)S(1)}, f32[4096,512]{0,1:T(8,128)}, u32[]{:S(2)}) copy-start(f32[4096,512]{0,1:T(8,128)} %get-tuple-element.229) | copy-start | bytes 25165828
  127.1 5.8 %copy-start.6 = (f32[512]{0:T(512)S(1)}, f32[512]{0:T(512)}, u32[]{:S(2)}) copy-start(f32[512]{0:T(512)} %param.33) | copy-start | bytes 6148
  127.1 5.8 %copy-start.7 = (f32[512]{0:T(512)S(1)}, f32[512]{0:T(512)}, u32[]{:S(2)}) copy-start(f32[512]{0:T(512)} %param.32) | copy-start | bytes 6148
  145.7 14.2 %copy-start.11 = (f32[512]{0:T(512)S(1)}, f32[512]{0:T(512)}, u32[]{:S(2)}) copy-start(f32[512]{0:T(512)} %param.37) | copy-start | bytes 6148
  145.7 14.2 %copy-start.12 = (f32[512]{0:T(512)S(1)}, f32[512]{0:T(512)}, u32[]{:S(2)}) copy-start(f32[512]{0:T(512)} %param.35) | copy-start | bytes 6148
  159.9 3.0 %copy-start.8 = (f32[512]{0:T(512)S(1)}, f32[512]{0:T(512)}, u32[]{:S(2)}) copy-start(f32[512]{0:T(512)} %param.39) | copy-start | bytes 6148
  159.9 3.0 %copy-start.9 = (f32[512]{0:T(512)S(1)}, f32[512]{0:T(512)}, u32[]{:S(2)}) copy-start(f32[512]{0:T(512)} %param.38) | copy-start | bytes 6148
